TPU v7x, 32 devices: a whole 2x2x4 slice. The times are simulated.
32 devices in a mesh: dp: 8 (over y, x, core), tensor: 4 (over z).
Axes of the slice: x: 2, y: 2, z: 4, core: 2. Of those that a mesh axis runs over, the one named last changes fastest.
Arguments:
- tokens: bfloat16 [16384, 2048], P(('dp', 'tensor')), may hold values from -6 to 6
- segments: int32 [8, 2048], P('dp'), may hold values from 0 to 7, never falling along the last dimension, each value on 1 to 1024 neighbouring positions
- ln_gain: float32 [2048], replicated, may hold values from 0.5 to 1.5
- ln_shift: float32 [2048], replicated, may hold values from -1.5 to 1.5
- qkv_weight: bfloat16 [2048, 3, 2048], P('dp', None, 'tensor'), may hold values from -0.125 to 0.125
- qkv_bias: float32 [3, 2048], P(None, 'tensor'), may hold values from -3 to 3
- out_weight: bfloat16 [2048, 2048], P('tensor', 'dp'), may hold values from -1 to 1
- out_bias: float32 [2048], replicated, may hold values from -3 to 3
- fc1_weight: bfloat16 [2048, 8192], P('dp', 'tensor'), may hold values from -0.125 to 0.125
- fc1_bias: float32 [8192], P('tensor'), may hold values from -3 to 3
- fc2_weight: bfloat16 [8192, 2048], P('tensor', 'dp'), may hold values from -0.0625 to 0.0625
- fc2_bias: float32 [2048], replicated, may hold values from -3 to 3
- cotangent: bfloat16 [16384, 2048], P(('dp', 'tensor')), may hold values from -6 to 6
Outputs:
- mixed: bfloat16 [16384, 2048], P(('dp', 'tensor'))
- input_grad: bfloat16 [16384, 2048], P(('dp', 'tensor'))
- qkv_weight_grad: float32 [2048, 3, 2048], P('dp', None, 'tensor')
- qkv_bias_grad: float32 [3, 2048], P(None, 'tensor')
- out_weight_grad: float32 [2048, 2048], P('tensor', 'dp')
- out_bias_grad: float32 [2048], replicated
- fc1_weight_grad: float32 [2048, 8192], P('dp', 'tensor')
- fc1_bias_grad: float32 [8192], P('tensor')
- fc2_weight_grad: float32 [8192, 2048], P('tensor', 'dp')
- fc2_bias_grad: float32 [2048], replicated
- gain_grad: float32 [2048], replicated
- shift_grad: float32 [2048], replicated
Inputs may be any that keep to these rules, and one draw needn't show every extreme that they name: `segments`: each row holds one data group's 2048 tokens; along a row the sequence numbers never fall, each sequence covers 1 to 1024 consecutive tokens, and some sequence covers exactly 1024.
All inputs are finite; a program needn't handle non-finite values.
Results may differ from a plain program's by a relative error of at most 0.013.
Values may be sent and summed in bfloat16 or wider, within the bound.
A program may use at most 320 MiB of HBM per device.

v0:
```python
import jax
import jax.numpy as jnp
from jax import lax
from jax.sharding import PartitionSpec as P

D = 2048
H = 32
HD = 64
ROT = 32
EPS = 1e-05
ROPE_BASE = 10000.0
NEGATIVE = -1e30


def contract_rows(left_op, right_op):
    return lax.dot_general(
        left_op, right_op, (((0,), (0,)), ((), ())), preferred_element_type=jnp.float32
    )


def contract_cols(left_op, right_op):
    return lax.dot_general(
        left_op, right_op, (((1,), (1,)), ((), ())), preferred_element_type=jnp.float32
    )


def gelu_tanh(values_in):
    return jax.nn.gelu(values_in, approximate=True)


def seq_positions(segment_row):
    row_count = segment_row.shape[0]
    row_index = jnp.arange(row_count, dtype=jnp.int32)
    seq_begins = jnp.concatenate([jnp.ones((1,), dtype=bool), segment_row[1:] != segment_row[:-1]])
    starts = lax.cummax(jnp.where(seq_begins, row_index, jnp.zeros_like(row_index)), axis=0)
    return row_index - starts


def rotary_tables(positions):
    half_rot = ROT // 2
    frequency = ROPE_BASE ** (-(jnp.arange(half_rot, dtype=jnp.float32) * 2.0) / ROT)
    angles = positions.astype(jnp.float32)[:, None] * frequency[None, :]
    return (jnp.cos(angles)[:, None, :], jnp.sin(angles)[:, None, :])


def rotate(heads_in, cosine_table, sine_table):
    half_rot = ROT // 2
    first_half = heads_in[..., :half_rot]
    second_half = heads_in[..., half_rot:ROT]
    return jnp.concatenate(
        [
            first_half * cosine_table - second_half * sine_table,
            second_half * cosine_table + first_half * sine_table,
            heads_in[..., ROT:],
        ],
        axis=-1,
    )


def allowed_block(segment_row, first_row, block_rows):
    key_count = segment_row.shape[0]
    query_index = first_row + jnp.arange(block_rows, dtype=jnp.int32)
    key_index = jnp.arange(key_count, dtype=jnp.int32)
    query_seg = lax.dynamic_slice_in_dim(segment_row, first_row, block_rows, 0)
    return (query_seg[:, None] == segment_row[None, :]) & (
        key_index[None, :] <= query_index[:, None]
    )


def attend(queries, key_rows, value_rows, segment_row, block_rows):
    group_rows = queries.shape[0]
    factor = HD ** (-0.5)

    def one_block(block_index):
        first_row = block_index * block_rows
        query_block = lax.dynamic_slice_in_dim(queries, first_row, block_rows, 0)
        raw_scores = (
            jnp.einsum("qhd,khd->hqk", query_block, key_rows, preferred_element_type=jnp.float32)
            * factor
        )
        allowed = allowed_block(segment_row, first_row, block_rows)
        scores = jnp.where(allowed[None], raw_scores, NEGATIVE)
        row_max = jnp.max(scores, axis=-1, keepdims=True)
        exponent = jnp.exp(scores - row_max)
        row_total = jnp.sum(exponent, axis=-1, keepdims=True)
        attn_probs = (exponent / row_total).astype(jnp.bfloat16)
        block_out = jnp.einsum(
            "hqk,khd->qhd", attn_probs, value_rows, preferred_element_type=jnp.float32
        )
        return (block_out, (row_max + jnp.log(row_total))[..., 0])

    block_out, log_norm = lax.map(one_block, jnp.arange(group_rows // block_rows, dtype=jnp.int32))
    return (block_out.reshape(group_rows, -1), log_norm)


def attend_back(queries, key_rows, value_rows, grad_mix, log_norm, segment_row, block_rows):
    group_rows = queries.shape[0]
    factor = HD ** (-0.5)

    def one_block(running, block_item):
        grad_keys, grad_values = running
        block_index, block_norm = block_item
        first_row = block_index * block_rows
        query_block = lax.dynamic_slice_in_dim(queries, first_row, block_rows, 0)
        grad_block = lax.dynamic_slice_in_dim(grad_mix, first_row, block_rows, 0)
        raw_scores = (
            jnp.einsum("qhd,khd->hqk", query_block, key_rows, preferred_element_type=jnp.float32)
            * factor
        )
        allowed = allowed_block(segment_row, first_row, block_rows)
        attn_probs = jnp.where(allowed[None], jnp.exp(raw_scores - block_norm[..., None]), 0.0)
        grad_values = grad_values + jnp.einsum(
            "hqk,qhd->khd",
            attn_probs.astype(jnp.bfloat16),
            grad_block,
            preferred_element_type=jnp.float32,
        )
        grad_probs = jnp.einsum(
            "qhd,khd->hqk", grad_block, value_rows, preferred_element_type=jnp.float32
        )
        inner = jnp.sum(attn_probs * grad_probs, axis=-1, keepdims=True)
        grad_scores = (attn_probs * (grad_probs - inner)).astype(jnp.bfloat16)
        grad_queries = (
            jnp.einsum("hqk,khd->qhd", grad_scores, key_rows, preferred_element_type=jnp.float32)
            * factor
        )
        grad_keys = (
            grad_keys
            + jnp.einsum(
                "hqk,qhd->khd", grad_scores, query_block, preferred_element_type=jnp.float32
            )
            * factor
        )
        return ((grad_keys, grad_values), grad_queries)

    zero_rows = jnp.zeros(queries.shape, jnp.float32)
    block_ids = jnp.arange(group_rows // block_rows, dtype=jnp.int32)
    (grad_keys, grad_values), grad_queries = lax.scan(
        one_block, (zero_rows, zero_rows), (block_ids, log_norm)
    )
    return (grad_queries.reshape(queries.shape), grad_keys, grad_values)


def local(
    tokens,
    segments,
    ln_gain,
    ln_shift,
    qkv_weight,
    qkv_bias,
    out_weight,
    out_bias,
    fc1_weight,
    fc1_bias,
    fc2_weight,
    fc2_bias,
    cotangent,
):
    heads_here = H // lax.axis_size("tensor")
    segment_row = segments[0]
    group_rows = segment_row.shape[0]
    block_rows = min(512, group_rows)
    x_local = tokens.astype(jnp.float32)
    row_mean = jnp.mean(x_local, axis=-1, keepdims=True)
    centred = x_local - row_mean
    inv_std = lax.rsqrt(jnp.mean(centred * centred, axis=-1, keepdims=True) + EPS)
    normalized = centred * inv_std
    normed = lax.all_gather(
        (normalized * ln_gain + ln_shift).astype(jnp.bfloat16), "tensor", axis=0, tiled=True
    )
    w_qkv, w_out, w_up, w_down = (
        lax.all_gather(qkv_weight, "dp", axis=0, tiled=True),
        lax.all_gather(out_weight, "dp", axis=1, tiled=True),
        lax.all_gather(fc1_weight, "dp", axis=0, tiled=True),
        lax.all_gather(fc2_weight, "dp", axis=1, tiled=True),
    )
    local_width = w_qkv.shape[2]
    flat_qkv = w_qkv.reshape(D, 3 * local_width)
    qkv_raw = jnp.dot(normed, flat_qkv, preferred_element_type=jnp.float32).reshape(
        group_rows, 3, local_width
    )
    qkv_raw = qkv_raw + qkv_bias[None]
    positions = seq_positions(segment_row)
    cosine_table, sine_table = rotary_tables(positions)
    queries = rotate(
        qkv_raw[:, 0].reshape(group_rows, heads_here, HD), cosine_table, sine_table
    ).astype(jnp.bfloat16)
    key_rows = rotate(
        qkv_raw[:, 1].reshape(group_rows, heads_here, HD), cosine_table, sine_table
    ).astype(jnp.bfloat16)
    value_rows = qkv_raw[:, 2].reshape(group_rows, heads_here, HD).astype(jnp.bfloat16)
    attended_f32, log_norm = attend(queries, key_rows, value_rows, segment_row, block_rows)
    attended = attended_f32.astype(jnp.bfloat16)
    hidden = jnp.dot(normed, w_up, preferred_element_type=jnp.float32) + fc1_bias
    activated = gelu_tanh(hidden).astype(jnp.bfloat16)
    block_sum = lax.psum_scatter(
        (
            jnp.dot(attended, w_out, preferred_element_type=jnp.float32)
            + jnp.dot(activated, w_down, preferred_element_type=jnp.float32)
        ).astype(jnp.bfloat16),
        "tensor",
        scatter_dimension=0,
        tiled=True,
    ).astype(jnp.float32)
    mixed = (x_local + block_sum + out_bias + fc2_bias).astype(jnp.bfloat16)
    w_qkv, w_out, w_up, w_down = (
        lax.all_gather(qkv_weight, "dp", axis=0, tiled=True),
        lax.all_gather(out_weight, "dp", axis=1, tiled=True),
        lax.all_gather(fc1_weight, "dp", axis=0, tiled=True),
        lax.all_gather(fc2_weight, "dp", axis=1, tiled=True),
    )
    flat_qkv = w_qkv.reshape(D, 3 * local_width)
    grad_full = lax.all_gather(cotangent, "tensor", axis=0, tiled=True)
    grad_act = contract_cols(grad_full, w_down)
    gelu_value, gelu_pull = jax.vjp(gelu_tanh, hidden)
    grad_hidden = gelu_pull(grad_act)[0].astype(jnp.bfloat16)
    grad_up = contract_rows(normed, grad_hidden)
    grad_up_bias = jnp.sum(grad_hidden.astype(jnp.float32), axis=0)
    grad_mix = (
        contract_cols(grad_full, w_out).astype(jnp.bfloat16).reshape(group_rows, heads_here, HD)
    )
    grad_queries, grad_keys, grad_values = attend_back(
        queries, key_rows, value_rows, grad_mix, log_norm, segment_row, block_rows
    )
    grad_qkv = jnp.stack(
        [
            rotate(grad_queries, cosine_table, -sine_table).reshape(group_rows, local_width),
            rotate(grad_keys, cosine_table, -sine_table).reshape(group_rows, local_width),
            grad_values.reshape(group_rows, local_width),
        ],
        axis=1,
    ).astype(jnp.bfloat16)
    grad_qkv_bias = jnp.sum(grad_qkv.astype(jnp.float32), axis=0)
    flat_grad = grad_qkv.reshape(group_rows, 3 * local_width)
    grad_qkv_w = contract_rows(normed, flat_grad).reshape(D, 3, local_width)
    grad_down = contract_rows(activated, grad_full)
    grad_out = contract_rows(attended, grad_full)
    summed_qkv, summed_out, summed_up, summed_down = (
        lax.psum_scatter(
            grad_qkv_w.astype(jnp.bfloat16), "dp", scatter_dimension=0, tiled=True
        ).astype(jnp.float32),
        lax.psum_scatter(
            grad_out.astype(jnp.bfloat16), "dp", scatter_dimension=1, tiled=True
        ).astype(jnp.float32),
        lax.psum_scatter(
            grad_up.astype(jnp.bfloat16), "dp", scatter_dimension=0, tiled=True
        ).astype(jnp.float32),
        lax.psum_scatter(
            grad_down.astype(jnp.bfloat16), "dp", scatter_dimension=1, tiled=True
        ).astype(jnp.float32),
    )
    grad_normed = lax.psum_scatter(
        (contract_cols(flat_grad, flat_qkv) + contract_cols(grad_hidden, w_up)).astype(
            jnp.bfloat16
        ),
        "tensor",
        scatter_dimension=0,
        tiled=True,
    ).astype(jnp.float32)
    grad_scaled = grad_normed * ln_gain
    input_grad = inv_std * (
        grad_scaled
        - jnp.mean(grad_scaled, axis=-1, keepdims=True)
        - normalized * jnp.mean(grad_scaled * normalized, axis=-1, keepdims=True)
    )
    input_grad = (input_grad + cotangent.astype(jnp.float32)).astype(jnp.bfloat16)
    gain_sum, shift_sum, output_sum = lax.psum(
        (
            jnp.sum(grad_normed * normalized, axis=0),
            jnp.sum(grad_normed, axis=0),
            jnp.sum(cotangent.astype(jnp.float32), axis=0),
        ),
        ("dp", "tensor"),
    )
    qkv_bias_sum, up_bias_sum = lax.psum((grad_qkv_bias, grad_up_bias), "dp")
    return (
        mixed,
        input_grad,
        summed_qkv,
        qkv_bias_sum,
        summed_out,
        output_sum,
        summed_up,
        up_bias_sum,
        summed_down,
        output_sum,
        gain_sum,
        shift_sum,
    )


def solution(mesh):
    in_specs = (
        P(("dp", "tensor"), None),
        P("dp", None),
        P(),
        P(),
        P("dp", None, "tensor"),
        P(None, "tensor"),
        P("tensor", "dp"),
        P(),
        P("dp", "tensor"),
        P("tensor"),
        P("tensor", "dp"),
        P(),
        P(("dp", "tensor"), None),
    )
    out_specs = (
        P(("dp", "tensor"), None),
        P(("dp", "tensor"), None),
        P("dp", None, "tensor"),
        P(None, "tensor"),
        P("tensor", "dp"),
        P(),
        P("dp", "tensor"),
        P("tensor"),
        P("tensor", "dp"),
        P(),
        P(),
        P(),
    )
    return jax.shard_map(local, mesh=mesh, in_specs=in_specs, out_specs=out_specs, check_vma=False)
```

profile of v0, /device:TPU:0, one launch (start us, length us, event | category | flops | bytes accessed | tf_op | source)
XLA Modules:
  0.0 1624.3 jit_solution(4911673076161956696)
XLA Ops:
  19.7 38.5 %all-gather.9.cloned.1.call-done = bf16[2048,3,512]{2,0,1:T(8,128)(2,1)} async-done(((bf16[256,3,512]{2,0,1:T(8,128)(2,1)}), bf16[2048,3,512]{2,0,1:T(8,128)(2,1)}) %all-gather.9.cloned.1.call-update) | async-done | bytes 6291472 | tf_op jit(solution)/shard_map/all_gather | solution.py:172
  67.0 143.0 %all-gather.7.cloned.1.call-done = bf16[2048,2048]{1,0:T(8,128)(2,1)} async-done(((bf16[512,2048]{1,0:T(8,128)(2,1)}), bf16[2048,2048]{1,0:T(8,128)(2,1)}) %all-gather.7.cloned.1.call-update) | async-done | bytes 8388624 | tf_op jit(solution)/shard_map/all_gather | solution.py:168
  210.0 17.8 %broadcast_add_fusion = f32[2048,3,512]{0,2,1:T(8,128)S(1)} fusion(f32[3,512]{1,0:T(4,128)S(1)} %copy-done.20, bf16[2048,3,512]{0,2,1:T(8,128)(2,1)} %copy.29, bf16[2048,2048]{1,0:T(8,128)(2,1)} %all-gather.7.cloned.1.call-done), kind=kOutput, calls=%fused_computation.66 | convolution fusion | flops 12888047616 | bytes 27269120 | tf_op jit(solution)/shard_map/dot_general | solution.py:179
  233.0 196.4 %while.27 = (s32[]{:T(128)}, bf16[4,512,8,64]{1,3,2,0:T(8,128)(2,1)}, f32[4,8,512]{2,1,0:T(8,128)S(1)}, s32[4]{0:T(128)S(1)}, s32[2048]{0:T(1024)S(1)}, /*index=...) while((s32[]{:T(128)}, ...), condition=%wide.region_7.8_spmd, body=%wide.region_4.7_spmd.sunk | while | flops 2251289088 | bytes 110774976 | solution.py:92
  439.4 528.9 %while.28 = (s32[]{:T(128)}, f32[2048,8,64]{0,2,1:T(8,128)}, f32[2048,8,64]{0,2,1:T(8,128)}, f32[4,512,8,64]{1,0,3,2:T(4,128)}, s32[4]{0:T(128)S(1)}, /*index=5*...) while((s32[]{:T(128)}, f32[2048,8,64]{0,2,1:T(8,128)}, ...), condition=%wide.region_11.12_spmd.clone, body=%wide.region_9.11_spmd.clone.sunk | while | flops 5452853760 | bytes 284264672 | solution.py:138
  442.1 18.6 %fusion.132 = f32[8,512,2048]{2,1,0:T(8,128)} fusion(bf16[2048,8,64]{0,2,1:T(8,128)(2,1)} %get-tuple-element.467, bf16[2048,8,64]{0,2,1:T(8,128)(2,1)} %get-tuple-element.466, s32[]{:T(128)S(6)} %select_n.49), kind=kOutput, calls=%fused_computation.29.clone.1 | convolution fusion | flops 1073741824 | bytes 36175876 | tf_op jit(solution)/shard_map/while/body/eval_jaxpr/qhd,khd->hqk/dot_general | solution.py:118
  460.7 25.0 %multiply_reduce_fusion.2 = (f32[8,512]{1,0:T(8,128)S(1)}, f32[8,512,2048]{2,1,0:T(8,128)}) fusion(f32[8,512,2048]{2,1,0:T(8,128)} %fusion.132, f32[8,512]{1,0:T(8,128)S(1)} %dynamic-slice_bitcast_fusion.2, bf16[2048,8,64]{0,2,1:T(8,128)(2,1)S(1)} %get-tuple-element.464, bf16[2048,8,64]{0,2,1:T(8,128)(2,1)} %get-tuple-element.461, ...), kind=kOutput, calls=%fused_computation.18.clone.1 | convolution fusion | flops 1115680768 | bytes 70811648 | tf_op jit(solution)/shard_map/while/body/eval_jaxpr/qhd,khd->hqk/dot_general | solution.py:107
  485.6 28.1 %multiply_convert_fusion.5 = bf16[8,512,2048]{2,1,0:T(8,128)(2,1)} fusion(f32[8,512,2048]{2,1,0:T(8,128)} %get-tuple-element.383, f32[8,512,2048]{2,1,0:T(8,128)} %fusion.132, f32[8,512]{1,0:T(8,128)S(1)} %get-tuple-element.384), kind=kLoop, calls=%fused_computation.17.clone.1 | loop fusion | flops 25165824 | bytes 83902464 | tf_op jit(solution)/shard_map/while/body/eval_jaxpr/convert_element_type | solution.py:122
  523.5 21.0 %dynamic_update_slice.19 = f32[4,512,8,64]{1,0,3,2:T(4,128)} dynamic-update-slice(f32[4,512,8,64]{1,0,3,2:T(4,128)} %get-tuple-element.443, f32[1,512,8,64]{1,0,3,2:T(1,128)S(1)} %copy.52, s32[]{:T(128)} %get-tuple-element.440, s32[]{:T(128)} %constant.48.clone.1..sunk.1, s32[]{:T(128)} %constant.48.clone.1..sunk.1, s32[]{:T(128)} %constant.48.clone.1..sunk.1) | dynamic-update-slice | bytes 2097156 | tf_op jit(solution)/shard_map/while/body/jit(dynamic_update_index_in_dim)/dynamic_update_slice | solution.py:92
  573.9 17.4 %fusion.132 = f32[8,512,2048]{2,1,0:T(8,128)} fusion(bf16[2048,8,64]{0,2,1:T(8,128)(2,1)} %get-tuple-element.467, bf16[2048,8,64]{0,2,1:T(8,128)(2,1)} %get-tuple-element.466, s32[]{:T(128)S(6)} %select_n.49), kind=kOutput, calls=%fused_computation.29.clone.1 | convolution fusion | flops 1073741824 | bytes 36175876 | tf_op jit(solution)/shard_map/while/body/eval_jaxpr/qhd,khd->hqk/dot_general | solution.py:118
  591.3 24.9 %multiply_reduce_fusion.2 = (f32[8,512]{1,0:T(8,128)S(1)}, f32[8,512,2048]{2,1,0:T(8,128)}) fusion(f32[8,512,2048]{2,1,0:T(8,128)} %fusion.132, f32[8,512]{1,0:T(8,128)S(1)} %dynamic-slice_bitcast_fusion.2, bf16[2048,8,64]{0,2,1:T(8,128)(2,1)S(1)} %get-tuple-element.464, bf16[2048,8,64]{0,2,1:T(8,128)(2,1)} %get-tuple-element.461, ...), kind=kOutput, calls=%fused_computation.18.clone.1 | convolution fusion | flops 1115680768 | bytes 70811648 | tf_op jit(solution)/shard_map/while/body/eval_jaxpr/qhd,khd->hqk/dot_general | solution.py:107
  616.1 27.4 %multiply_convert_fusion.5 = bf16[8,512,2048]{2,1,0:T(8,128)(2,1)} fusion(f32[8,512,2048]{2,1,0:T(8,128)} %get-tuple-element.383, f32[8,512,2048]{2,1,0:T(8,128)} %fusion.132, f32[8,512]{1,0:T(8,128)S(1)} %get-tuple-element.384), kind=kLoop, calls=%fused_computation.17.clone.1 | loop fusion | flops 25165824 | bytes 83902464 | tf_op jit(solution)/shard_map/while/body/eval_jaxpr/convert_element_type | solution.py:122
  653.3 21.0 %dynamic_update_slice.19 = f32[4,512,8,64]{1,0,3,2:T(4,128)} dynamic-update-slice(f32[4,512,8,64]{1,0,3,2:T(4,128)} %get-tuple-element.443, f32[1,512,8,64]{1,0,3,2:T(1,128)S(1)} %copy.52, s32[]{:T(128)} %get-tuple-element.440, s32[]{:T(128)} %constant.48.clone.1..sunk.1, s32[]{:T(128)} %constant.48.clone.1..sunk.1, s32[]{:T(128)} %constant.48.clone.1..sunk.1) | dynamic-update-slice | bytes 2097156 | tf_op jit(solution)/shard_map/while/body/jit(dynamic_update_index_in_dim)/dynamic_update_slice | solution.py:92
  723.4 24.9 %multiply_reduce_fusion.2 = (f32[8,512]{1,0:T(8,128)S(1)}, f32[8,512,2048]{2,1,0:T(8,128)}) fusion(f32[8,512,2048]{2,1,0:T(8,128)} %fusion.132, f32[8,512]{1,0:T(8,128)S(1)} %dynamic-slice_bitcast_fusion.2, bf16[2048,8,64]{0,2,1:T(8,128)(2,1)S(1)} %get-tuple-element.464, bf16[2048,8,64]{0,2,1:T(8,128)(2,1)} %get-tuple-element.461, ...), kind=kOutput, calls=%fused_computation.18.clone.1 | convolution fusion | flops 1115680768 | bytes 70811648 | tf_op jit(solution)/shard_map/while/body/eval_jaxpr/qhd,khd->hqk/dot_general | solution.py:107
  748.3 27.4 %multiply_convert_fusion.5 = bf16[8,512,2048]{2,1,0:T(8,128)(2,1)} fusion(f32[8,512,2048]{2,1,0:T(8,128)} %get-tuple-element.383, f32[8,512,2048]{2,1,0:T(8,128)} %fusion.132, f32[8,512]{1,0:T(8,128)S(1)} %get-tuple-element.384), kind=kLoop, calls=%fused_computation.17.clone.1 | loop fusion | flops 25165824 | bytes 83902464 | tf_op jit(solution)/shard_map/while/body/eval_jaxpr/convert_element_type | solution.py:122
  785.5 21.0 %dynamic_update_slice.19 = f32[4,512,8,64]{1,0,3,2:T(4,128)} dynamic-update-slice(f32[4,512,8,64]{1,0,3,2:T(4,128)} %get-tuple-element.443, f32[1,512,8,64]{1,0,3,2:T(1,128)S(1)} %copy.52, s32[]{:T(128)} %get-tuple-element.440, s32[]{:T(128)} %constant.48.clone.1..sunk.1, s32[]{:T(128)} %constant.48.clone.1..sunk.1, s32[]{:T(128)} %constant.48.clone.1..sunk.1) | dynamic-update-slice | bytes 2097156 | tf_op jit(solution)/shard_map/while/body/jit(dynamic_update_index_in_dim)/dynamic_update_slice | solution.py:92
  838.2 17.4 %fusion.132 = f32[8,512,2048]{2,1,0:T(8,128)} fusion(bf16[2048,8,64]{0,2,1:T(8,128)(2,1)} %get-tuple-element.467, bf16[2048,8,64]{0,2,1:T(8,128)(2,1)} %get-tuple-element.466, s32[]{:T(128)S(6)} %select_n.49), kind=kOutput, calls=%fused_computation.29.clone.1 | convolution fusion | flops 1073741824 | bytes 36175876 | tf_op jit(solution)/shard_map/while/body/eval_jaxpr/qhd,khd->hqk/dot_general | solution.py:118
  855.6 24.9 %multiply_reduce_fusion.2 = (f32[8,512]{1,0:T(8,128)S(1)}, f32[8,512,2048]{2,1,0:T(8,128)}) fusion(f32[8,512,2048]{2,1,0:T(8,128)} %fusion.132, f32[8,512]{1,0:T(8,128)S(1)} %dynamic-slice_bitcast_fusion.2, bf16[2048,8,64]{0,2,1:T(8,128)(2,1)S(1)} %get-tuple-element.464, bf16[2048,8,64]{0,2,1:T(8,128)(2,1)} %get-tuple-element.461, ...), kind=kOutput, calls=%fused_computation.18.clone.1 | convolution fusion | flops 1115680768 | bytes 70811648 | tf_op jit(solution)/shard_map/while/body/eval_jaxpr/qhd,khd->hqk/dot_general | solution.py:107
  880.5 27.4 %multiply_convert_fusion.5 = bf16[8,512,2048]{2,1,0:T(8,128)(2,1)} fusion(f32[8,512,2048]{2,1,0:T(8,128)} %get-tuple-element.383, f32[8,512,2048]{2,1,0:T(8,128)} %fusion.132, f32[8,512]{1,0:T(8,128)S(1)} %get-tuple-element.384), kind=kLoop, calls=%fused_computation.17.clone.1 | loop fusion | flops 25165824 | bytes 83902464 | tf_op jit(solution)/shard_map/while/body/eval_jaxpr/convert_element_type | solution.py:122
  917.7 21.0 %dynamic_update_slice.19 = f32[4,512,8,64]{1,0,3,2:T(4,128)} dynamic-update-slice(f32[4,512,8,64]{1,0,3,2:T(4,128)} %get-tuple-element.443, f32[1,512,8,64]{1,0,3,2:T(1,128)S(1)} %copy.52, s32[]{:T(128)} %get-tuple-element.440, s32[]{:T(128)} %constant.48.clone.1..sunk.1, s32[]{:T(128)} %constant.48.clone.1..sunk.1, s32[]{:T(128)} %constant.48.clone.1..sunk.1) | dynamic-update-slice | bytes 2097156 | tf_op jit(solution)/shard_map/while/body/jit(dynamic_update_index_in_dim)/dynamic_update_slice | solution.py:92
  1019.1 19.3 %fusion.51 = bf16[2048,3,512]{2,0,1:T(8,128)(2,1)} fusion(bf16[2048,3,512]{0,2,1:T(8,128)(2,1)} %copy.35, bf16[2048,2048]{1,0:T(8,128)(2,1)} %all-gather.7.cloned.1.call-done), kind=kOutput, calls=%fused_computation.79 | convolution fusion | flops 12888047616 | bytes 20971520 | tf_op jit(solution)/shard_map/dot_general | solution.py:16
  1038.6 24.4 %fusion.72 = f32[2048,2048]{1,0:T(8,128)} fusion(bf16[2048,2048]{1,0:T(8,128)(2,1)} %all-gather.7.cloned.1.call-done, bf16[2048,2048]{1,0:T(8,128)(2,1)} %all-gather.13.cloned.1.call-done), kind=kOutput, calls=%fused_computation.124 | convolution fusion | flops 17179869184 | bytes 33554432 | tf_op jit(solution)/shard_map/dot_general | solution.py:194
  1063.0 36.4 %convert_reduce_fusion = (f32[2048]{0:T(1024)}, bf16[2048,2048]{1,0:T(8,128)(2,1)}) fusion(f32[2048,2048]{1,0:T(8,128)} %fusion.72, f32[2048]{0:T(1024)S(1)} %copy-done.21, bf16[2048,2048]{1,0:T(8,128)(2,1)} %all-gather.17.cloned.1.call-done, bf16[2048,2048]{1,0:T(8,128)(2,1)} %all-gather.15.cloned.1.call-done), kind=kOutput, calls=%fused_computation.50 | convolution fusion | flops 17276336128 | bytes 41959424 | tf_op jit(solution)/shard_map/dot_general | solution.py:22
  1099.4 24.1 %convolution_convert_fusion.1 = bf16[2048,2048]{1,0:T(8,128)(2,1)} fusion(bf16[2048,2048]{1,0:T(8,128)(2,1)} %all-gather.7.cloned.1.call-done, bf16[2048,2048]{1,0:T(8,128)(2,1)} %get-tuple-element.220), kind=kOutput, calls=%fused_computation.60 | convolution fusion | flops 17184063488 | bytes 25165824 | tf_op jit(solution)/shard_map/dot_general | solution.py:16
  1123.5 27.1 %convolution_convert_fusion = bf16[2048,2048]{1,0:T(8,128)(2,1)} fusion(bf16[2048,2048]{1,0:T(8,128)(2,1)} %all-gather.17.cloned.1.call-done, f32[2048,2048]{1,0:T(8,128)} %fusion.72, f32[2048]{0:T(1024)S(1)} %copy-done.21), kind=kOutput, calls=%fused_computation.59 | convolution fusion | flops 17226006528 | bytes 33562624 | tf_op jit(solution)/shard_map/dot_general | solution.py:16
  1150.7 20.6 %fusion.73 = f32[2048,2048,1]{1,0,2:T(8,128)} fusion(bf16[2048,3,512]{2,0,1:T(8,128)(2,1)} %get-tuple-element.222, bf16[2048,3,512]{2,0,1:T(8,128)(2,1)} %all-gather.9.cloned.1.call-done), kind=kOutput, calls=%fused_computation.125 | convolution fusion | flops 12884901888 | bytes 29360128 | tf_op jit(solution)/shard_map/dot_general | solution.py:22
  1171.3 25.6 %fusion.33 = bf16[2048,2048]{1,0:T(8,128)(2,1)} fusion(f32[2048,2048,1]{1,0,2:T(8,128)} %fusion.73, bf16[2048,2048]{1,0:T(8,128)(2,1)} %get-tuple-element.220, bf16[2048,2048]{1,0:T(8,128)(2,1)} %all-gather.13.cloned.1.call-done), kind=kOutput, calls=%fused_computation.49 | convolution fusion | flops 17188257792 | bytes 41943040 | tf_op jit(solution)/shard_map/dot_general | solution.py:22
  1208.6 31.4 %add_convert_fusion = bf16[2048,2048]{1,0:T(8,128)(2,1)} fusion(f32[2048,2048]{1,0:T(8,128)} %fusion.71, bf16[2048,2048]{1,0:T(8,128)(2,1)} %all-gather.15.cloned.1.call-done, f32[2048,2048]{1,0:T(8,128)} %fusion.72, f32[2048]{0:T(1024)S(1)} %copy-done.21), kind=kOutput, calls=%fused_computation.51 | convolution fusion | flops 17230200832 | bytes 50339840 | tf_op jit(solution)/shard_map/dot_general | solution.py:199
  1240.7 24.5 %all-reduce.1 = (f32[3,512]{1,0:T(4,128)}, f32[2048]{0:T(1024)}) all-reduce(f32[3,512]{1,0:T(4,128)S(1)} %copy-done.15, f32[2048]{0:T(1024)S(1)} %copy-done.16), channel_id=1, replica_groups=mesh['dp'=8,'tensor'=4] {'dp'}, use_global_device_ids=true, to_apply=%region_17.18 | all-reduce | flops 3584 | bytes 28672 | tf_op jit(solution)/shard_map/psum | solution.py:275
  1277.0 144.1 %reduce-scatter.9.cloned.1.call-done = bf16[512,2048]{1,0:T(8,128)(2,1)} async-done(((bf16[2048,2048]{1,0:T(8,128)(2,1)}), bf16[512,2048]{1,0:T(8,128)(2,1)}) %reduce-scatter.9.cloned.1.call-update) | async-done | bytes 2097168 | tf_op jit(solution)/shard_map/reduce_scatter | solution.py:252
  1424.6 143.9 %reduce-scatter.7.cloned.1.call-done = bf16[512,2048]{1,0:T(8,128)(2,1)} async-done(((bf16[2048,2048]{1,0:T(8,128)(2,1)}), bf16[512,2048]{1,0:T(8,128)(2,1)}) %reduce-scatter.7.cloned.1.call-update) | async-done | bytes 2097168 | tf_op jit(solution)/shard_map/reduce_scatter | solution.py:196
  1575.1 41.5 %all-reduce = (f32[2048]{0:T(1024)S(1)}, f32[2048]{0:T(1024)}, f32[2048]{0:T(1024)}) all-reduce(f32[2048]{0:T(1024)S(1)} %get-tuple-element.237, f32[2048]{0:T(1024)S(1)} %get-tuple-element.168, f32[2048]{0:T(1024)S(1)} %get-tuple-element.171), channel_id=1, replica_groups=mesh['dp'=8,'tensor'=4] {'dp','tensor'}, use_global_device_ids=true, to_apply=%region_20.21 | all-reduce | flops 6144 | bytes 49152 | tf_op jit(solution)/shard_map/psum | solution.py:267
  (198 shorter events, 493.8 us)
Async XLA Ops:
  7.2 5.1 copy-start
  7.2 51.0 %all-gather.9.cloned.1.call-start = ((), (), s32[]{:S(2)}) async-start(), calls=%async_computation.7 | async-start | bytes 7077888 | tf_op jit(solution)/shard_map/all_gather | solution.py:172
  7.9 202.1 %all-gather.7.cloned.1.call-start = ((), (), s32[]{:S(2)}) async-start(), calls=%async_computation.6 | async-start | bytes 10485760 | tf_op jit(solution)/shard_map/all_gather | solution.py:168
  9.9 7.7 copy-start.11
  9.9 7.8 copy-start.6
  12.2 6.2 copy-start.13
  15.1 414.3 %all-gather.11.cloned.1.call-start = ((), (), s32[]{:S(2)}) async-start(), calls=%async_computation.8 | async-start | bytes 2359296 | tf_op jit(solution)/shard_map/all_gather | solution.py:173
  15.9 413.6 %all-gather.17.cloned.1.call-start = ((), (), s32[]{:S(2)}) async-start(), calls=%async_computation.12 | async-start | bytes 10485760 | tf_op jit(solution)/shard_map/all_gather | solution.py:213
  16.5 1022.1 %all-gather.13.cloned.1.call-start = ((), (), s32[]{:S(2)}) async-start(), calls=%async_computation.9 | async-start | bytes 9437184 | tf_op jit(solution)/shard_map/all_gather | solution.py:174
  17.0 1045.9 %all-gather.15.cloned.1.call-start = ((), (), s32[]{:S(2)}) async-start(), calls=%async_computation.10 | async-start | bytes 9437184 | tf_op jit(solution)/shard_map/all_gather | solution.py:175
  17.6 1247.6 %reduce-scatter.13.cloned.1.call-start = ((), (), s32[]{:S(2)}) async-start(), calls=%async_computation.15 | async-start | bytes 2359296 | tf_op jit(solution)/shard_map/reduce_scatter | solution.py:242
  19.7 211.1 %copy-start.7 = (f32[2048,16]{0,1:T(8,128)}, f32[2048,16]{0,1:T(8,128)S(1)}, u32[]{:S(2)}) copy-start(f32[2048,16]{0,1:T(8,128)S(1)} %get-tuple-element.246) | copy-start | bytes 393220
  19.7 190.3 %copy-start.20 = (f32[3,512]{1,0:T(4,128)S(1)}, f32[3,512]{1,0:T(4,128)}, u32[]{:S(2)}) copy-start(f32[3,512]{1,0:T(4,128)} %param.22) | copy-start | bytes 18436
  968.3 9.6 copy-start.8
  968.3 9.6 copy-start.9
  991.5 5.3 copy-start.2
  991.5 5.3 copy-start.3
  1001.1 9.0 copy-start.4
  1019.1 247.9 %reduce-scatter.11.cloned.1.call-start = ((), (), s32[]{:S(2)}) async-start(), calls=%async_computation.14 | async-start | bytes 7077888 | tf_op jit(solution)/shard_map/reduce_scatter | solution.py:239
  1038.5 24.5 %copy-start.21 = (f32[2048]{0:T(1024)S(1)}, f32[2048]{0:T(1024)}, u32[]{:S(2)}) copy-start(f32[2048]{0:T(1024)} %param.26) | copy-start | bytes 24580
  1038.5 231.0 %reduce-scatter.15.cloned.1.call-start = ((), (), s32[]{:S(2)}) async-start(), calls=%async_computation.16 | async-start | bytes 9437184 | tf_op jit(solution)/shard_map/reduce_scatter | solution.py:245
  1123.5 150.8 %reduce-scatter.17.cloned.1.call-start = ((), (), s32[]{:S(2)}) async-start(), calls=%async_computation.17 | async-start | bytes 9437184 | tf_op jit(solution)/shard_map/reduce_scatter | solution.py:248
  1150.6 270.4 %reduce-scatter.9.cloned.1.call-start = ((), (), s32[]{:S(2)}) async-start(), calls=%async_computation.13 | async-start | bytes 10485760 | tf_op jit(solution)/shard_map/reduce_scatter | solution.py:252
  1196.9 1.6 copy-start.5
  1196.9 371.6 %reduce-scatter.7.cloned.1.call-start = ((), (), s32[]{:S(2)}) async-start(), calls=%async_computation.11 | async-start | bytes 10485760 | tf_op jit(solution)/shard_map/reduce_scatter | solution.py:196
  1240.0 0.7 copy-start.16
  1240.0 181.1 %copy-start.1 = (bf16[512,2048]{1,0:T(8,128)(2,1)S(1)}, bf16[512,2048]{1,0:T(8,128)(2,1)}, u32[]{:S(2)}) copy-start(bf16[512,2048]{1,0:T(8,128)(2,1)} %param.17) | copy-start | bytes 6291460
  1240.0 181.0 %copy-start.10 = (f32[2048]{0:T(1024)S(1)}, f32[2048]{0:T(1024)}, u32[]{:S(2)}) copy-start(f32[2048]{0:T(1024)} %param.19) | copy-start | bytes 24580
  1240.1 181.0 %copy-start.12 = (f32[512]{0:T(512)S(1)}, f32[512]{0:T(512)}, u32[]{:S(2)}) copy-start(f32[512]{0:T(512)} %copy-done.11) | copy-start | bytes 6148
  1240.1 181.0 %copy-start.14 = (f32[512]{0:T(512)S(1)}, f32[512]{0:T(512)}, u32[]{:S(2)}) copy-start(f32[512]{0:T(512)} %copy-done.13) | copy-start | bytes 6148
  1267.0 301.5 %copy-start.18 = (f32[2048]{0:T(1024)S(1)}, f32[2048]{0:T(1024)}, u32[]{:S(2)}) copy-start(f32[2048]{0:T(1024)} %param.28) | copy-start | bytes 24580
  1267.0 301.5 %copy-start.19 = (f32[2048]{0:T(1024)S(1)}, f32[2048]{0:T(1024)}, u32[]{:S(2)}) copy-start(f32[2048]{0:T(1024)} %param.24) | copy-start | bytes 24580
  (2 other events, 1.3 us)
Sparse Core Ops, SparseCore 0:
  9.9 48.2 all-gather.8
  60.3 149.6 all-gather.6
  211.9 26.4 all-gather.10
  239.8 149.6 all-gather.16
  391.2 52.6 all-gather.12
  445.6 55.9 all-gather.14
  1019.2 39.2 reduce-scatter.12
  1062.3 61.7 reduce-scatter.10
  1127.5 71.2 reduce-scatter.14
  1202.5 71.6 reduce-scatter.16
  1276.6 144.4 reduce-scatter.8
  1423.3 145.1 reduce-scatter.6
where the time goes:
time: 1640 us; the launch traced here: 1620 us
  matrix products  701 us (43%)
  waiting for transfers between devices  475 us (29%)
  other arithmetic  221 us (13%)
  local copies, waits for them, and re-layouts  141 us (9%)
  blocking collectives  66 us (4%)
    dot_general x8, matrix products, one_block(): jnp.einsum('qhd,khd->hqk', query_block, key_rows, preferred_element_type=...  161 us
    reduce_scatter x1, waiting for transfers between devices, local(): lax.psum_scatter((contract_cols(flat_grad, flat_qkv) + contract_cols(grad...  144 us
    reduce_scatter x1, waiting for transfers between devices, local(): lax.psum_scatter((jnp.dot(attended, w_out, preferred_element_type=jnp.flo...  144 us
    all_gather x1, waiting for transfers between devices, local(): lax.all_gather((normalized * ln_gain + ln_shift).astype(jnp.bfloat16), 't...  143 us
    convert_element_type x4, other arithmetic, one_block(): grad_scores = (attn_probs * (grad_probs - inner)).astype(jnp.bfloat16)  110 us
    dot_general x4, matrix products, contract_cols(): lax.dot_general(left_op, right_op, (((1,), (1,)), ((), ())), preferred_el...  92.6 us
    dynamic_update_slice x8, local copies, waits for them, and re-layouts, attend(): lax.map(one_block, jnp.arange(group_rows // block_rows, dtype=jnp.int32))  88.3 us
    dot_general x4, matrix products, contract_rows(): lax.dot_general(left_op, right_op, (((0,), (0,)), ((), ())), preferred_el...  79.5 us
  transfers between devices with their start and end apart: 12, of which 5 were waited for; matrix products, arithmetic and copies ran while one was open for 65% of the time, Pallas kernels for 0%

commit v1 on v0

--- a/solution.py
+++ b/solution.py
@@ -10,6 +10,27 @@
 EPS = 1e-05
 ROPE_BASE = 10000.0
 NEGATIVE = -1e30
+
+
+def collect(x, axis, dim):
+    length, position, span = (lax.axis_size(axis), lax.axis_index(axis), x.shape[dim])
+    forward = [(i, (i + 1) % length) for i in range(length)]
+    behind = [(i, (i - 1) % length) for i in range(length)]
+    filled = jnp.zeros((*x.shape[:dim], length * span, *x.shape[dim + 1 :]), x.dtype)
+    filled = lax.dynamic_update_slice_in_dim(filled, x, position * span, axis=dim)
+    from_left = from_right = x
+    half = length // 2
+    for step in range(1, half + 1):
+        from_left = lax.ppermute(from_left, axis, forward)
+        filled = lax.dynamic_update_slice_in_dim(
+            filled, from_left, (position - step) % length * span, axis=dim
+        )
+        if step < length - half:
+            from_right = lax.ppermute(from_right, axis, behind)
+            filled = lax.dynamic_update_slice_in_dim(
+                filled, from_right, (position + step) % length * span, axis=dim
+            )
+    return filled
 
 
 def contract_rows(left_op, right_op):
@@ -165,9 +186,7 @@
     centred = x_local - row_mean
     inv_std = lax.rsqrt(jnp.mean(centred * centred, axis=-1, keepdims=True) + EPS)
     normalized = centred * inv_std
-    normed = lax.all_gather(
-        (normalized * ln_gain + ln_shift).astype(jnp.bfloat16), "tensor", axis=0, tiled=True
-    )
+    normed = collect((normalized * ln_gain + ln_shift).astype(jnp.bfloat16), "tensor", 0)
     w_qkv, w_out, w_up, w_down = (
         lax.all_gather(qkv_weight, "dp", axis=0, tiled=True),
         lax.all_gather(out_weight, "dp", axis=1, tiled=True),

time: 1640 us -> 1700 us (1.037)
  waiting for transfers between devices: 475 us -> 507 us
  local copies, waits for them, and re-layouts: 141 us -> 170 us
    ppermute x0 -> x3, waiting for transfers between devices: none -> 166 us  [the longest x2 114 us: collect(): from_left = lax.ppermute(from_left, axis, forward)]
    all_gather x1 -> x0, waiting for transfers between devices: 143 us -> none  [local(): lax.all_gather((normalized * ln_gain + ln_shift).astype(jnp.bfloat16), 't...]
    reduce_scatter x1, waiting for transfers between devices: 1.95 us -> 50.8 us  [local(): lax.psum_scatter(grad_down.astype(jnp.bfloat16), 'dp', scatter_dimension=...]
    all_gather x1, waiting for transfers between devices: 38.5 us -> 0.01 us  [local(): lax.all_gather(qkv_weight, 'dp', axis=0, tiled=True)]
  transfers between devices with their start and end apart: 12 -> 14, of which waited for: 5 -> 6; matrix products, arithmetic and copies ran while one was open for 65% -> 64% of each run, Pallas kernels for 0% -> 0%
where the time goes in v1:
time: 1700 us
  matrix products  705 us (41%)
  waiting for transfers between devices  507 us (30%)
  other arithmetic  223 us (13%)
  local copies, waits for them, and re-layouts  170 us (10%)
  blocking collectives  64.5 us (4%)
    dot_general x8, matrix products, one_block(): jnp.einsum('qhd,khd->hqk', query_block, key_rows, preferred_element_type=...  160 us
    reduce_scatter x1, waiting for transfers between devices, local(): lax.psum_scatter((jnp.dot(attended, w_out, preferred_element_type=jnp.flo...  144 us
    reduce_scatter x1, waiting for transfers between devices, local(): lax.psum_scatter((contract_cols(flat_grad, flat_qkv) + contract_cols(grad...  144 us
    ppermute x2, waiting for transfers between devices, collect(): from_left = lax.ppermute(from_left, axis, forward)  114 us
    convert_element_type x4, other arithmetic, one_block(): grad_scores = (attn_probs * (grad_probs - inner)).astype(jnp.bfloat16)  110 us
    dot_general x4, matrix products, contract_cols(): lax.dot_general(left_op, right_op, (((1,), (1,)), ((), ())), preferred_el...  91.1 us
    dynamic_update_slice x8, local copies, waits for them, and re-layouts, attend(): lax.map(one_block, jnp.arange(group_rows // block_rows, dtype=jnp.int32))  88.3 us
    dot_general x4, matrix products, contract_rows(): lax.dot_general(left_op, right_op, (((0,), (0,)), ((), ())), preferred_el...  78.7 us
  transfers between devices with their start and end apart: 14, of which 6 were waited for; matrix products, arithmetic and copies ran while one was open for 64% of the time, Pallas kernels for 0%

profile of v1, /device:TPU:0, one launch (start us, length us, event | category | flops | bytes accessed | tf_op | source)
XLA Modules:
  0.0 1696.3 jit_solution(8363502954862662522)
XLA Ops:
  20.0 46.8 %collective-permute-done = bf16[512,2048]{1,0:T(8,128)(2,1)} collective-permute-done((bf16[512,2048]{1,0:T(8,128)(2,1)}, bf16[512,2048]{1,0:T(8,128)(2,1)}, u32[]{:S(2)}, u32[]{:S(2)}) %collective-permute-start) | collective-permute-done | bytes 2097184 | tf_op jit(solution)/shard_map/ppermute | solution.py:24
  81.0 51.5 %collective-permute-done.1 = bf16[512,2048]{1,0:T(8,128)(2,1)} collective-permute-done((bf16[512,2048]{1,0:T(8,128)(2,1)}, bf16[512,2048]{1,0:T(8,128)(2,1)}, u32[]{:S(2)}, u32[]{:S(2)}) %collective-permute-start.1) | collective-permute-done | bytes 2097184 | tf_op jit(solution)/shard_map/ppermute | solution.py:29
  141.0 67.4 %collective-permute-done.2 = bf16[512,2048]{1,0:T(8,128)(2,1)} collective-permute-done((bf16[512,2048]{1,0:T(8,128)(2,1)}, bf16[512,2048]{1,0:T(8,128)(2,1)}, u32[]{:S(2)}, u32[]{:S(2)}) %collective-permute-start.2) | collective-permute-done | bytes 2097184 | tf_op jit(solution)/shard_map/ppermute | solution.py:24
  221.7 29.9 %broadcast_add_fusion = f32[2048,3,512]{0,2,1:T(8,128)S(1)} fusion(f32[3,512]{1,0:T(4,128)S(1)} %copy-done.21, bf16[2048,3,512]{0,2,1:T(8,128)(2,1)} %copy.37, bf16[2048,2048]{0,1:T(8,128)(2,1)} %constant_dynamic-update-slice_fusion), kind=kOutput, calls=%fused_computation.66 | convolution fusion | flops 12888047616 | bytes 27269120 | tf_op jit(solution)/shard_map/dot_general | solution.py:198
  256.9 194.8 %while.27 = (s32[]{:T(128)}, bf16[4,512,8,64]{1,3,2,0:T(8,128)(2,1)}, f32[4,8,512]{2,1,0:T(8,128)S(1)}, s32[4]{0:T(128)S(1)}, s32[2048]{0:T(1024)S(1)}, /*index=...) while((s32[]{:T(128)}, ...), condition=%wide.region_7.8_spmd, body=%wide.region_4.7_spmd.sunk | while | flops 2251289088 | bytes 110774480 | solution.py:113
  466.7 526.7 %while.28 = (s32[]{:T(128)}, f32[2048,8,64]{0,2,1:T(8,128)}, f32[2048,8,64]{0,2,1:T(8,128)}, f32[4,512,8,64]{1,0,3,2:T(4,128)}, s32[4]{0:T(128)S(1)}, /*index=5*...) while((s32[]{:T(128)}, f32[2048,8,64]{0,2,1:T(8,128)}, ...), condition=%wide.region_11.12_spmd.clone, body=%wide.region_9.11_spmd.clone.sunk | while | flops 5452853760 | bytes 284264704 | solution.py:159
  487.0 24.8 %multiply_reduce_fusion.2 = (f32[8,512]{1,0:T(8,128)S(1)}, f32[8,512,2048]{2,1,0:T(8,128)}) fusion(f32[8,512,2048]{2,1,0:T(8,128)} %fusion.132, f32[8,512]{1,0:T(8,128)S(1)} %dynamic-slice_bitcast_fusion.2, bf16[2048,8,64]{0,2,1:T(8,128)(2,1)S(1)} %get-tuple-element.464, bf16[2048,8,64]{0,2,1:T(8,128)(2,1)} %get-tuple-element.461, ...), kind=kOutput, calls=%fused_computation.18.clone.1 | convolution fusion | flops 1115680768 | bytes 70811648 | tf_op jit(solution)/shard_map/while/body/eval_jaxpr/qhd,khd->hqk/dot_general | solution.py:128
  511.8 27.4 %multiply_convert_fusion.5 = bf16[8,512,2048]{2,1,0:T(8,128)(2,1)} fusion(f32[8,512,2048]{2,1,0:T(8,128)} %get-tuple-element.383, f32[8,512,2048]{2,1,0:T(8,128)} %fusion.132, f32[8,512]{1,0:T(8,128)S(1)} %get-tuple-element.384), kind=kLoop, calls=%fused_computation.17.clone.1 | loop fusion | flops 25165824 | bytes 83902464 | tf_op jit(solution)/shard_map/while/body/eval_jaxpr/convert_element_type | solution.py:143
  575.9 21.0 %dynamic_update_slice.39 = f32[4,512,8,64]{1,0,3,2:T(4,128)} dynamic-update-slice(f32[4,512,8,64]{1,0,3,2:T(4,128)} %get-tuple-element.443, f32[1,512,8,64]{1,0,3,2:T(1,128)S(1)} %copy.60, s32[]{:T(128)S(6)} %copy.81, s32[]{:T(128)} %constant.71.clone.1..sunk.1, s32[]{:T(128)} %constant.71.clone.1..sunk.1, s32[]{:T(128)} %constant.71.clone.1..sunk.1) | dynamic-update-slice | bytes 2097156 | tf_op jit(solution)/shard_map/while/body/jit(dynamic_update_index_in_dim)/dynamic_update_slice | solution.py:113
  598.1 17.4 %fusion.132 = f32[8,512,2048]{2,1,0:T(8,128)} fusion(bf16[2048,8,64]{0,2,1:T(8,128)(2,1)} %get-tuple-element.467, bf16[2048,8,64]{0,2,1:T(8,128)(2,1)} %get-tuple-element.466, s32[]{:T(128)S(6)} %select_n.83), kind=kOutput, calls=%fused_computation.29.clone.1 | convolution fusion | flops 1073741824 | bytes 36175876 | tf_op jit(solution)/shard_map/while/body/eval_jaxpr/qhd,khd->hqk/dot_general | solution.py:139
  616.8 24.8 %multiply_reduce_fusion.2 = (f32[8,512]{1,0:T(8,128)S(1)}, f32[8,512,2048]{2,1,0:T(8,128)}) fusion(f32[8,512,2048]{2,1,0:T(8,128)} %fusion.132, f32[8,512]{1,0:T(8,128)S(1)} %dynamic-slice_bitcast_fusion.2, bf16[2048,8,64]{0,2,1:T(8,128)(2,1)S(1)} %get-tuple-element.464, bf16[2048,8,64]{0,2,1:T(8,128)(2,1)} %get-tuple-element.461, ...), kind=kOutput, calls=%fused_computation.18.clone.1 | convolution fusion | flops 1115680768 | bytes 70811648 | tf_op jit(solution)/shard_map/while/body/eval_jaxpr/qhd,khd->hqk/dot_general | solution.py:128
  641.6 27.4 %multiply_convert_fusion.5 = bf16[8,512,2048]{2,1,0:T(8,128)(2,1)} fusion(f32[8,512,2048]{2,1,0:T(8,128)} %get-tuple-element.383, f32[8,512,2048]{2,1,0:T(8,128)} %fusion.132, f32[8,512]{1,0:T(8,128)S(1)} %get-tuple-element.384), kind=kLoop, calls=%fused_computation.17.clone.1 | loop fusion | flops 25165824 | bytes 83902464 | tf_op jit(solution)/shard_map/while/body/eval_jaxpr/convert_element_type | solution.py:143
  708.0 21.0 %dynamic_update_slice.39 = f32[4,512,8,64]{1,0,3,2:T(4,128)} dynamic-update-slice(f32[4,512,8,64]{1,0,3,2:T(4,128)} %get-tuple-element.443, f32[1,512,8,64]{1,0,3,2:T(1,128)S(1)} %copy.60, s32[]{:T(128)S(6)} %copy.81, s32[]{:T(128)} %constant.71.clone.1..sunk.1, s32[]{:T(128)} %constant.71.clone.1..sunk.1, s32[]{:T(128)} %constant.71.clone.1..sunk.1) | dynamic-update-slice | bytes 2097156 | tf_op jit(solution)/shard_map/while/body/jit(dynamic_update_index_in_dim)/dynamic_update_slice | solution.py:113
  748.9 24.8 %multiply_reduce_fusion.2 = (f32[8,512]{1,0:T(8,128)S(1)}, f32[8,512,2048]{2,1,0:T(8,128)}) fusion(f32[8,512,2048]{2,1,0:T(8,128)} %fusion.132, f32[8,512]{1,0:T(8,128)S(1)} %dynamic-slice_bitcast_fusion.2, bf16[2048,8,64]{0,2,1:T(8,128)(2,1)S(1)} %get-tuple-element.464, bf16[2048,8,64]{0,2,1:T(8,128)(2,1)} %get-tuple-element.461, ...), kind=kOutput, calls=%fused_computation.18.clone.1 | convolution fusion | flops 1115680768 | bytes 70811648 | tf_op jit(solution)/shard_map/while/body/eval_jaxpr/qhd,khd->hqk/dot_general | solution.py:128
  773.7 27.4 %multiply_convert_fusion.5 = bf16[8,512,2048]{2,1,0:T(8,128)(2,1)} fusion(f32[8,512,2048]{2,1,0:T(8,128)} %get-tuple-element.383, f32[8,512,2048]{2,1,0:T(8,128)} %fusion.132, f32[8,512]{1,0:T(8,128)S(1)} %get-tuple-element.384), kind=kLoop, calls=%fused_computation.17.clone.1 | loop fusion | flops 25165824 | bytes 83902464 | tf_op jit(solution)/shard_map/while/body/eval_jaxpr/convert_element_type | solution.py:143
  840.1 21.0 %dynamic_update_slice.39 = f32[4,512,8,64]{1,0,3,2:T(4,128)} dynamic-update-slice(f32[4,512,8,64]{1,0,3,2:T(4,128)} %get-tuple-element.443, f32[1,512,8,64]{1,0,3,2:T(1,128)S(1)} %copy.60, s32[]{:T(128)S(6)} %copy.81, s32[]{:T(128)} %constant.71.clone.1..sunk.1, s32[]{:T(128)} %constant.71.clone.1..sunk.1, s32[]{:T(128)} %constant.71.clone.1..sunk.1) | dynamic-update-slice | bytes 2097156 | tf_op jit(solution)/shard_map/while/body/jit(dynamic_update_index_in_dim)/dynamic_update_slice | solution.py:113
  881.0 24.8 %multiply_reduce_fusion.2 = (f32[8,512]{1,0:T(8,128)S(1)}, f32[8,512,2048]{2,1,0:T(8,128)}) fusion(f32[8,512,2048]{2,1,0:T(8,128)} %fusion.132, f32[8,512]{1,0:T(8,128)S(1)} %dynamic-slice_bitcast_fusion.2, bf16[2048,8,64]{0,2,1:T(8,128)(2,1)S(1)} %get-tuple-element.464, bf16[2048,8,64]{0,2,1:T(8,128)(2,1)} %get-tuple-element.461, ...), kind=kOutput, calls=%fused_computation.18.clone.1 | convolution fusion | flops 1115680768 | bytes 70811648 | tf_op jit(solution)/shard_map/while/body/eval_jaxpr/qhd,khd->hqk/dot_general | solution.py:128
  905.8 27.4 %multiply_convert_fusion.5 = bf16[8,512,2048]{2,1,0:T(8,128)(2,1)} fusion(f32[8,512,2048]{2,1,0:T(8,128)} %get-tuple-element.383, f32[8,512,2048]{2,1,0:T(8,128)} %fusion.132, f32[8,512]{1,0:T(8,128)S(1)} %get-tuple-element.384), kind=kLoop, calls=%fused_computation.17.clone.1 | loop fusion | flops 25165824 | bytes 83902464 | tf_op jit(solution)/shard_map/while/body/eval_jaxpr/convert_element_type | solution.py:143
  972.2 21.0 %dynamic_update_slice.39 = f32[4,512,8,64]{1,0,3,2:T(4,128)} dynamic-update-slice(f32[4,512,8,64]{1,0,3,2:T(4,128)} %get-tuple-element.443, f32[1,512,8,64]{1,0,3,2:T(1,128)S(1)} %copy.60, s32[]{:T(128)S(6)} %copy.81, s32[]{:T(128)} %constant.71.clone.1..sunk.1, s32[]{:T(128)} %constant.71.clone.1..sunk.1, s32[]{:T(128)} %constant.71.clone.1..sunk.1) | dynamic-update-slice | bytes 2097156 | tf_op jit(solution)/shard_map/while/body/jit(dynamic_update_index_in_dim)/dynamic_update_slice | solution.py:113
  1047.8 18.7 %fusion.51 = bf16[2048,3,512]{2,0,1:T(8,128)(2,1)} fusion(bf16[2048,3,512]{0,2,1:T(8,128)(2,1)} %copy.44, bf16[2048,2048]{0,1:T(8,128)(2,1)} %constant_dynamic-update-slice_fusion), kind=kOutput, calls=%fused_computation.79 | convolution fusion | flops 12888047616 | bytes 20971520 | tf_op jit(solution)/shard_map/dot_general | solution.py:37
  1066.7 24.7 %fusion.72 = f32[2048,2048]{1,0:T(8,128)} fusion(bf16[2048,2048]{0,1:T(8,128)(2,1)} %constant_dynamic-update-slice_fusion, bf16[2048,2048]{1,0:T(8,128)(2,1)} %all-gather.10.cloned.1.call-done), kind=kOutput, calls=%fused_computation.128 | convolution fusion | flops 17179869184 | bytes 33554432 | tf_op jit(solution)/shard_map/dot_general | solution.py:213
  1091.3 36.3 %convert_reduce_fusion = (f32[2048]{0:T(1024)}, bf16[2048,2048]{1,0:T(8,128)(2,1)}) fusion(f32[2048,2048]{1,0:T(8,128)} %fusion.72, f32[2048]{0:T(1024)S(1)} %copy-done.22, bf16[2048,2048]{1,0:T(8,128)(2,1)} %all-gather.14.cloned.1.call-done, bf16[2048,2048]{1,0:T(8,128)(2,1)} %all-gather.12.cloned.1.call-done), kind=kOutput, calls=%fused_computation.50 | convolution fusion | flops 17276336128 | bytes 41959424 | tf_op jit(solution)/shard_map/dot_general | solution.py:43
  1127.7 23.9 %convolution_convert_fusion.1 = bf16[2048,2048]{1,0:T(8,128)(2,1)} fusion(bf16[2048,2048]{0,1:T(8,128)(2,1)} %constant_dynamic-update-slice_fusion, bf16[2048,2048]{1,0:T(8,128)(2,1)} %get-tuple-element.220), kind=kOutput, calls=%fused_computation.60 | convolution fusion | flops 17184063488 | bytes 25165824 | tf_op jit(solution)/shard_map/dot_general | solution.py:37
  1151.6 27.1 %convolution_convert_fusion = bf16[2048,2048]{1,0:T(8,128)(2,1)} fusion(bf16[2048,2048]{1,0:T(8,128)(2,1)} %all-gather.14.cloned.1.call-done, f32[2048,2048]{1,0:T(8,128)} %fusion.72, f32[2048]{0:T(1024)S(1)} %copy-done.22), kind=kOutput, calls=%fused_computation.59 | convolution fusion | flops 17226006528 | bytes 33562624 | tf_op jit(solution)/shard_map/dot_general | solution.py:37
  1178.7 19.5 %fusion.73 = f32[2048,2048,1]{1,0,2:T(8,128)} fusion(bf16[2048,3,512]{2,0,1:T(8,128)(2,1)} %get-tuple-element.222, bf16[2048,3,512]{2,0,1:T(8,128)(2,1)} %all-gather.6.cloned.1.call-done), kind=kOutput, calls=%fused_computation.129 | convolution fusion | flops 12884901888 | bytes 29360128 | tf_op jit(solution)/shard_map/dot_general | solution.py:43
  1198.2 25.4 %fusion.33 = bf16[2048,2048]{1,0:T(8,128)(2,1)} fusion(f32[2048,2048,1]{1,0,2:T(8,128)} %fusion.73, bf16[2048,2048]{1,0:T(8,128)(2,1)} %get-tuple-element.220, bf16[2048,2048]{1,0:T(8,128)(2,1)} %all-gather.10.cloned.1.call-done), kind=kOutput, calls=%fused_computation.49 | convolution fusion | flops 17188257792 | bytes 41943040 | tf_op jit(solution)/shard_map/dot_general | solution.py:43
  1236.0 28.8 %add_convert_fusion = bf16[2048,2048]{1,0:T(8,128)(2,1)} fusion(f32[2048,2048]{1,0:T(8,128)} %fusion.71, bf16[2048,2048]{1,0:T(8,128)(2,1)} %all-gather.12.cloned.1.call-done, f32[2048,2048]{1,0:T(8,128)} %fusion.72, f32[2048]{0:T(1024)S(1)} %copy-done.22), kind=kOutput, calls=%fused_computation.51 | convolution fusion | flops 17230200832 | bytes 50339840 | tf_op jit(solution)/shard_map/dot_general | solution.py:218
  1265.4 23.0 %all-reduce.1 = (f32[3,512]{1,0:T(4,128)}, f32[2048]{0:T(1024)}) all-reduce(f32[3,512]{1,0:T(4,128)S(1)} %copy-done.15, f32[2048]{0:T(1024)S(1)} %copy-done.17), channel_id=1, replica_groups=mesh['dp'=8,'tensor'=4] {'dp'}, use_global_device_ids=true, to_apply=%region_17.18 | all-reduce | flops 3584 | bytes 28672 | tf_op jit(solution)/shard_map/psum | solution.py:294
  1295.7 50.8 %reduce-scatter.17.cloned.1.call-done = bf16[2048,256]{1,0:T(8,128)(2,1)} async-done(((bf16[2048,2048]{1,0:T(8,128)(2,1)}), bf16[2048,256]{1,0:T(8,128)(2,1)}) %reduce-scatter.17.cloned.1.call-update) | async-done | bytes 1048592 | tf_op jit(solution)/shard_map/reduce_scatter | solution.py:267
  1349.2 144.0 %reduce-scatter.9.cloned.1.call-done = bf16[512,2048]{1,0:T(8,128)(2,1)} async-done(((bf16[2048,2048]{1,0:T(8,128)(2,1)}), bf16[512,2048]{1,0:T(8,128)(2,1)}) %reduce-scatter.9.cloned.1.call-update) | async-done | bytes 2097168 | tf_op jit(solution)/shard_map/reduce_scatter | solution.py:271
  1496.7 144.1 %reduce-scatter.7.cloned.1.call-done = bf16[512,2048]{1,0:T(8,128)(2,1)} async-done(((bf16[2048,2048]{1,0:T(8,128)(2,1)}), bf16[512,2048]{1,0:T(8,128)(2,1)}) %reduce-scatter.7.cloned.1.call-update) | async-done | bytes 2097168 | tf_op jit(solution)/shard_map/reduce_scatter | solution.py:215
  1647.4 41.5 %all-reduce = (f32[2048]{0:T(1024)S(1)}, f32[2048]{0:T(1024)}, f32[2048]{0:T(1024)}) all-reduce(f32[2048]{0:T(1024)S(1)} %get-tuple-element.237, f32[2048]{0:T(1024)S(1)} %get-tuple-element.168, f32[2048]{0:T(1024)S(1)} %get-tuple-element.171), channel_id=1, replica_groups=mesh['dp'=8,'tensor'=4] {'dp','tensor'}, use_global_device_ids=true, to_apply=%region_20.21 | all-reduce | flops 6144 | bytes 49152 | tf_op jit(solution)/shard_map/psum | solution.py:286
  (212 shorter events, 562.1 us)
Async XLA Ops:
  7.2 5.5 copy-start.16
  7.2 5.5 copy-start.9
  7.2 205.6 %all-gather.6.cloned.1.call-start = ((), (), s32[]{:S(2)}) async-start(), calls=%async_computation.6 | async-start | bytes 7077888 | tf_op jit(solution)/shard_map/all_gather | solution.py:191
  7.9 448.9 %all-gather.8.cloned.1.call-start = ((), (), s32[]{:S(2)}) async-start(), calls=%async_computation.7 | async-start | bytes 2359296 | tf_op jit(solution)/shard_map/all_gather | solution.py:192
  8.7 448.2 %all-gather.14.cloned.1.call-start = ((), (), s32[]{:S(2)}) async-start(), calls=%async_computation.11 | async-start | bytes 10485760 | tf_op jit(solution)/shard_map/all_gather | solution.py:232
  9.4 1057.2 %all-gather.10.cloned.1.call-start = ((), (), s32[]{:S(2)}) async-start(), calls=%async_computation.8 | async-start | bytes 9437184 | tf_op jit(solution)/shard_map/all_gather | solution.py:193
  10.0 1081.3 %all-gather.12.cloned.1.call-start = ((), (), s32[]{:S(2)}) async-start(), calls=%async_computation.9 | async-start | bytes 9437184 | tf_op jit(solution)/shard_map/all_gather | solution.py:194
  12.0 58.2 %copy-start.5 = (s32[1,2048]{1,0:T(1,128)S(1)}, s32[1,2048]{1,0:T(1,128)}, u32[]{:S(2)}) copy-start(s32[1,2048]{1,0:T(1,128)} %param.18) | copy-start | bytes 24580
  12.0 63.3 %copy-start.11 = (f32[512]{0:T(512)}, f32[512]{0:T(512)S(1)}, u32[]{:S(2)}) copy-start(f32[512]{0:T(512)S(1)} %broadcast_multiply_fusion.2) | copy-start | bytes 6148
  12.8 58.0 %copy-start.13 = (f32[512]{0:T(512)}, f32[512]{0:T(512)S(1)}, u32[]{:S(2)}) copy-start(f32[512]{0:T(512)S(1)} %add_rsqrt_fusion) | copy-start | bytes 6148
  14.9 51.9 %collective-permute-start = (bf16[512,2048]{1,0:T(8,128)(2,1)}, bf16[512,2048]{1,0:T(8,128)(2,1)}, u32[]{:S(2)}, u32[]{:S(2)}) collective-permute-start(bf16[512,2048]{1,0:T(8,128)(2,1)} %fusion.57), channel_id=1, source_target_pairs={{0,1},{1,2},{2,3},{3,0},{4,5},{5,6},{6,7},{7,4},{8,9},{9,10},{10,1... | collective-permute-start | bytes 6291464 | tf_op jit(solution)/shard_map/ppermute | solution.py:24
  17.9 114.5 %collective-permute-start.1 = (bf16[512,2048]{1,0:T(8,128)(2,1)}, bf16[512,2048]{1,0:T(8,128)(2,1)}, u32[]{:S(2)}, u32[]{:S(2)}) collective-permute-start(bf16[512,2048]{1,0:T(8,128)(2,1)} %fusion.57), channel_id=1, source_target_pairs={{0,3},{1,0},{2,1},{3,2},{4,7},{5,4},{6,5},{7,6},{8,11},{9,8},{10,9... | collective-permute-start | bytes 6291464 | tf_op jit(solution)/shard_map/ppermute | solution.py:29
  66.8 141.6 %collective-permute-start.2 = (bf16[512,2048]{1,0:T(8,128)(2,1)}, bf16[512,2048]{1,0:T(8,128)(2,1)}, u32[]{:S(2)}, u32[]{:S(2)}) collective-permute-start(bf16[512,2048]{1,0:T(8,128)(2,1)} %collective-permute-done), channel_id=1, source_target_pairs={{0,1},{1,2},{2,3},{3,0},{4,5},{5,6},{6,7},{7,4},{8,9},{9,10},{10,1... | collective-permute-start | bytes 6291464 | tf_op jit(solution)/shard_map/ppermute | solution.py:24
  66.8 1221.7 %reduce-scatter.13.cloned.1.call-start = ((), (), s32[]{:S(2)}) async-start(), calls=%async_computation.14 | async-start | bytes 2359296 | tf_op jit(solution)/shard_map/reduce_scatter | solution.py:261
  78.0 176.7 %copy-start.6 = (f32[2048,16]{0,1:T(8,128)}, f32[2048,16]{0,1:T(8,128)S(1)}, u32[]{:S(2)}) copy-start(f32[2048,16]{0,1:T(8,128)S(1)} %get-tuple-element.246) | copy-start | bytes 393220
  212.8 8.9 copy-start.21
  996.8 10.7 copy-start.7
  996.8 10.7 copy-start.8
  1005.6 5.6 copy-start.2
  1029.8 9.0 copy-start.3
  1047.8 242.6 %reduce-scatter.11.cloned.1.call-start = ((), (), s32[]{:S(2)}) async-start(), calls=%async_computation.13 | async-start | bytes 7077888 | tf_op jit(solution)/shard_map/reduce_scatter | solution.py:258
  1066.6 24.8 %copy-start.22 = (f32[2048]{0:T(1024)S(1)}, f32[2048]{0:T(1024)}, u32[]{:S(2)}) copy-start(f32[2048]{0:T(1024)} %param.26) | copy-start | bytes 24580
  1066.6 226.3 %reduce-scatter.15.cloned.1.call-start = ((), (), s32[]{:S(2)}) async-start(), calls=%async_computation.15 | async-start | bytes 9437184 | tf_op jit(solution)/shard_map/reduce_scatter | solution.py:264
  1151.5 195.0 %reduce-scatter.17.cloned.1.call-start = ((), (), s32[]{:S(2)}) async-start(), calls=%async_computation.16 | async-start | bytes 9437184 | tf_op jit(solution)/shard_map/reduce_scatter | solution.py:267
  1178.7 314.5 %reduce-scatter.9.cloned.1.call-start = ((), (), s32[]{:S(2)}) async-start(), calls=%async_computation.12 | async-start | bytes 10485760 | tf_op jit(solution)/shard_map/reduce_scatter | solution.py:271
  1223.7 417.1 %reduce-scatter.7.cloned.1.call-start = ((), (), s32[]{:S(2)}) async-start(), calls=%async_computation.10 | async-start | bytes 10485760 | tf_op jit(solution)/shard_map/reduce_scatter | solution.py:215
  1264.7 228.5 %copy-start.1 = (bf16[512,2048]{1,0:T(8,128)(2,1)S(1)}, bf16[512,2048]{1,0:T(8,128)(2,1)}, u32[]{:S(2)}) copy-start(bf16[512,2048]{1,0:T(8,128)(2,1)} %param.17) | copy-start | bytes 6291460
  1264.8 228.5 %copy-start.10 = (f32[2048]{0:T(1024)S(1)}, f32[2048]{0:T(1024)}, u32[]{:S(2)}) copy-start(f32[2048]{0:T(1024)} %param.19) | copy-start | bytes 24580
  1264.8 228.4 %copy-start.12 = (f32[512]{0:T(512)S(1)}, f32[512]{0:T(512)}, u32[]{:S(2)}) copy-start(f32[512]{0:T(512)} %copy-done.11) | copy-start | bytes 6148
  1264.8 228.4 %copy-start.14 = (f32[512]{0:T(512)S(1)}, f32[512]{0:T(512)}, u32[]{:S(2)}) copy-start(f32[512]{0:T(512)} %copy-done.13) | copy-start | bytes 6148
  1290.3 350.5 %copy-start.19 = (f32[2048]{0:T(1024)S(1)}, f32[2048]{0:T(1024)}, u32[]{:S(2)}) copy-start(f32[2048]{0:T(1024)} %param.28) | copy-start | bytes 24580
  1290.3 350.5 %copy-start.20 = (f32[2048]{0:T(1024)S(1)}, f32[2048]{0:T(1024)}, u32[]{:S(2)}) copy-start(f32[2048]{0:T(1024)} %param.24) | copy-start | bytes 24580
  (5 other events, 9.0 us)
Sparse Core Ops, SparseCore 0:
  9.9 48.2 all-gather.5
  60.1 28.1 all-gather.7
  89.9 201.1 all-gather.13
  292.9 53.5 all-gather.9
  348.2 55.9 all-gather.11
  1047.9 82.5 reduce-scatter.12
  1134.3 61.7 reduce-scatter.10
  1199.6 71.2 reduce-scatter.14
  1274.7 71.7 reduce-scatter.16
  1348.7 144.4 reduce-scatter.8
  1495.6 145.1 reduce-scatter.6
